TPU v7x, 32 devices: a whole 2x2x4 slice. The times are simulated.
32 devices in a mesh: expert: 8 (over y, x, core), dp: 4 (over z).
Axes of the slice: x: 2, y: 2, z: 4, core: 2. Of those that a mesh axis runs over, the one named last changes fastest.
Arguments:
- tokens: bfloat16 [4096, 2048], P(('expert', 'dp')), may hold values from -6 to 6
- expert_ids: int32 [4096, 4], P(('expert', 'dp')), may hold values from 0 to 15, all different within a row; in each aligned block of 128 rows (0 to 127, 128 to 255, ...) at most 96 rows name the same one
- gate_probs: float32 [4096, 4], P(('expert', 'dp')), may hold values from 0.05 to 0.5
- expert_weights: bfloat16 [2048, 3, 16, 384], P(None, None, 'expert'), may hold values from -0.125 to 0.125
- out_grad: bfloat16 [4096, 2048], P(('expert', 'dp')), may hold values from -1.5 to 1.5
Outputs:
- layer_out: bfloat16 [4096, 2048], P(('expert', 'dp'))
- token_grad: bfloat16 [4096, 2048], P(('expert', 'dp'))
- gate_grad: float32 [4096, 4], P(('expert', 'dp'))
- weight_grad: float32 [2048, 3, 16, 384], P('dp', None, 'expert')
Inputs may be any that keep to these rules, and one draw needn't show every extreme that they name: `expert_ids`: each row names 4 different experts. Among the 128 rows of one device (aligned blocks of rows), no expert is named by more than 96 rows, and in some block some expert is named by exactly 96 rows.
All inputs are finite; a program needn't handle non-finite values.
Results may differ from a plain program's by a relative error of at most 0.0085.
Values may be sent and summed in bfloat16 or wider, within the bound.
A program may use at most 128 MiB of HBM per device.

v0:
```python
import jax
import jax.numpy as jnp
from jax import lax
from jax.sharding import PartitionSpec as P

F32 = jnp.float32
BF16 = jnp.bfloat16


def dot(a, b, ca, cb):
    return lax.dot_general(a, b, (((ca,), (cb,)), ((), ())), preferred_element_type=F32)


def local(tokens, expert_ids, gate_probs, expert_weights, out_grad):
    tok_count, top_count = expert_ids.shape
    d = tokens.shape[1]
    ranks = lax.axis_size("expert")
    me = lax.axis_index("expert")
    local_experts, h = expert_weights.shape[2:]
    n = ranks * tok_count
    eh = local_experts * h
    x = lax.all_gather(tokens, "expert", axis=0, tiled=True)
    small = jnp.concatenate([expert_ids.astype(F32), gate_probs], axis=1)
    small = lax.all_gather(small, "expert", axis=0, tiled=True)
    g = lax.all_gather(out_grad, "expert", axis=0, tiled=True)
    ids = small[:, :top_count].astype(jnp.int32)
    probs = small[:, top_count:]
    mine = me * local_experts + jnp.arange(local_experts, dtype=jnp.int32)
    hit = ids[:, :, None] == mine[None, None, :]
    p = jnp.sum(jnp.where(hit, probs[:, :, None], 0.0), axis=1)
    w = expert_weights.reshape(d, 3 * eh)
    wgu = w[:, : 2 * eh]
    wd = w[:, 2 * eh :]
    a = dot(x, wgu, 1, 0)
    gate = a[:, :eh].reshape(n, local_experts, h)
    up = a[:, eh:].reshape(n, local_experts, h)
    s = jax.nn.sigmoid(gate)
    hidden = gate * s * up
    ph = (p[:, :, None] * hidden).astype(BF16).reshape(n, eh)
    lpart = dot(ph, wd, 1, 1).astype(BF16)
    layer_out = lax.psum_scatter(lpart, "expert", scatter_dimension=0, tiled=True)
    wd_grad = dot(g, ph, 0, 0).astype(BF16)
    wd_grad = lax.psum_scatter(wd_grad, "dp", scatter_dimension=0, tiled=True)
    u = dot(g, wd, 1, 0).reshape(n, local_experts, h)
    gg = jnp.sum(u * hidden, axis=-1)
    hc = p[:, :, None] * u
    gc = (hc * up * s * (1.0 + gate * (1.0 - s))).astype(BF16).reshape(n, eh)
    uc = (hc * gate * s).astype(BF16).reshape(n, eh)
    cots = jnp.concatenate([gc, uc], axis=1)
    tpart = dot(cots, wgu, 1, 1).astype(BF16)
    token_grad = lax.psum_scatter(tpart, "expert", scatter_dimension=0, tiled=True)
    ggk = jnp.sum(jnp.where(hit, gg[:, None, :], 0.0), axis=2)
    gate_grad = lax.psum_scatter(ggk, "expert", scatter_dimension=0, tiled=True)
    wgu_grad = dot(x, cots, 0, 0).astype(BF16)
    wgu_grad = lax.psum_scatter(wgu_grad, "dp", scatter_dimension=0, tiled=True)
    wg = jnp.concatenate([wgu_grad, wd_grad], axis=1)
    weight_grad = wg.astype(F32).reshape(-1, 3, local_experts, h)
    return (layer_out, token_grad, gate_grad, weight_grad)


def solution(mesh):
    tok = P(("expert", "dp"), None)
    wsp = P(None, None, "expert", None)
    return jax.shard_map(
        local,
        mesh=mesh,
        in_specs=(tok, tok, tok, wsp, tok),
        out_specs=(tok, tok, tok, P("dp", None, "expert", None)),
        check_vma=False,
    )
```

profile of v0, /device:TPU:0, one launch (start us, length us, event | category | flops | bytes accessed | tf_op | source)
XLA Modules:
  0.0 438.3 jit_solution(9271335342334902050)
XLA Ops:
  8.7 20.9 %reshape.38 = bf16[2048,2304]{1,0:T(8,128)(2,1)} reshape(bf16[2048,3,2,384]{3,2,1,0:T(2,128)(2,1)} %param.8) | data formatting | bytes 18874368 | tf_op jit(solution)/shard_map/reshape | solution.py:31
  29.6 10.5 %all_gather.9 = f32[1024,8]{0,1:T(8,128)S(1)} all-gather(f32[128,8]{0,1:T(8,128)S(1)} %pad_maximum_fusion.4), channel_id=1, replica_groups=mesh['expert'=8,'dp'=4] {'expert'}, dimensions={0}, use_global_device_ids=true | all-gather | bytes 36864 | tf_op jit(solution)/shard_map/all_gather | solution.py:24
  40.1 9.2 %all-gather.3.cloned.1.call-done = bf16[1024,2048]{1,0:T(8,128)(2,1)} async-done(((bf16[128,2048]{1,0:T(8,128)(2,1)}), bf16[1024,2048]{1,0:T(8,128)(2,1)}) %all-gather.3.cloned.1.call-update) | async-done | bytes 4194320 | tf_op jit(solution)/shard_map/all_gather | solution.py:22
  49.4 10.0 %fusion.3 = f32[1024,1536]{1,0:T(8,128)S(1)} fusion(bf16[1024,2048]{1,0:T(8,128)(2,1)} %all-gather.3.cloned.1.call-done, bf16[2048,2304]{1,0:T(8,128)(2,1)} %reshape.38), kind=kOutput, calls=%fused_computation.4 | convolution fusion | flops 6442450944 | bytes 16777216 | tf_op jit(solution)/shard_map/dot_general | solution.py:11
  59.4 3.5 fusion.16
  62.9 1.6 copy-done
  64.5 2.4 copy.35
  66.9 2.5 copy.37
  69.3 2.4 copy.38
  71.7 2.4 copy.39
  74.1 13.9 %all-gather.5.cloned.1.call-done = bf16[1024,2048]{1,0:T(8,128)(2,1)} async-done(((bf16[128,2048]{1,0:T(8,128)(2,1)}), bf16[1024,2048]{1,0:T(8,128)(2,1)}) %all-gather.5.cloned.1.call-update) | async-done | bytes 4194320 | tf_op jit(solution)/shard_map/all_gather | solution.py:25
  88.0 6.3 %fusion.9 = f32[1024,768]{0,1:T(8,128)S(1)} fusion(bf16[1024,2048]{1,0:T(8,128)(2,1)} %all-gather.5.cloned.1.call-done, bf16[2048,2304]{1,0:T(8,128)(2,1)} %reshape.38), kind=kOutput, calls=%fused_computation.16 | convolution fusion | flops 3221225472 | bytes 10485760 | tf_op jit(solution)/shard_map/dot_general | solution.py:11
  94.3 2.4 copy.34
  96.7 2.4 copy.40
  99.1 4.8 %multiply_reduce_fusion = f32[1024,2]{0,1:T(2,128)S(1)} fusion(f32[1024,2,384]{2,0,1:T(8,128)} %copy.40, f32[1024,2,384]{2,0,1:T(8,128)} %copy.39, f32[1024,2,384]{2,0,1:T(8,128)} %copy.37), kind=kLoop, calls=%fused_computation.10 | loop fusion | flops 5502976 | bytes 9445376 | tf_op jit(solution)/shard_map/reduce_sum | solution.py:45
  104.2 2.4 mul.62
  106.7 1.9 copy.47
  109.9 6.0 %multiply_convert_fusion.1 = (bf16[1024,768]{1,0:T(8,128)(2,1)}, bf16[1024,768]{1,0:T(8,128)(2,1)}, bf16[1024,768]{1,0:T(8,128)(2,1)S(1)}) fusion(f32[1024,768]{1,0:T(8,128)} %bitcast.22, f32[1024,768]{1,0:T(8,128)S(1)} %copy-done.1, f32[1024,1536]{1,0:T(8,128)} %copy-done), kind=kLoop, calls=%fused_computation.12 | loop fusion | flops 14155776 | bytes 17301504 | tf_op jit(solution)/shard_map/convert_element_type | solution.py:47
  115.9 1.1 copy-done.2
  117.1 4.8 %fusion.8 = bf16[2048,768]{0,1:T(8,128)(2,1)} fusion(bf16[1024,768]{1,0:T(8,128)(2,1)S(1)} %get-tuple-element.32, bf16[1024,2048]{1,0:T(8,128)(2,1)S(1)} %copy-done.8), kind=kOutput, calls=%fused_computation.15 | convolution fusion | flops 3222798336 | bytes 8912896 | tf_op jit(solution)/shard_map/dot_general | solution.py:11
  122.0 1.3 copy-done.4
  123.8 10.9 %fusion = bf16[2048,1536]{0,1:T(8,128)(2,1)} fusion(bf16[1024,2048]{1,0:T(8,128)(2,1)} %all-gather.3.cloned.1.call-done, bf16[1024,768]{1,0:T(8,128)(2,1)S(1)} %copy-done.5, bf16[1024,768]{1,0:T(8,128)(2,1)S(1)} %copy-done.4), kind=kOutput, calls=%fused_computation.1 | convolution fusion | flops 6451888128 | bytes 13631488 | tf_op jit(solution)/shard_map/dot_general | solution.py:11
  134.8 11.0 %fusion.5 = bf16[1024,2048]{1,0:T(8,128)(2,1)} fusion(bf16[2048,2304]{1,0:T(8,128)(2,1)} %reshape.38, bf16[1024,768]{1,0:T(8,128)(2,1)S(1)} %copy-done.5, bf16[1024,768]{1,0:T(8,128)(2,1)S(1)} %copy-done.4), kind=kOutput, calls=%fused_computation.6 | convolution fusion | flops 6450839552 | bytes 13631488 | tf_op jit(solution)/shard_map/dot_general | solution.py:11
  145.8 1.3 copy-done.3
  147.2 6.9 %convolution_convert_fusion.1 = bf16[1024,2048]{1,0:T(8,128)(2,1)} fusion(bf16[1024,768]{1,0:T(8,128)(2,1)S(1)} %copy-done.3, bf16[2048,2304]{1,0:T(8,128)(2,1)} %reshape.38), kind=kOutput, calls=%fused_computation.7 | convolution fusion | flops 3223322624 | bytes 8912896 | tf_op jit(solution)/shard_map/dot_general | solution.py:11
  154.1 1.5 copy.45
  155.6 51.5 %reduce-scatter.14.cloned.1.call-done = bf16[512,768]{0,1:T(8,128)(2,1)} async-done(((bf16[2048,768]{0,1:T(8,128)(2,1)}), bf16[512,768]{0,1:T(8,128)(2,1)}) %reduce-scatter.14.cloned.1.call-update) | async-done | bytes 786448 | tf_op jit(solution)/shard_map/reduce_scatter | solution.py:43
  207.1 113.1 %reduce-scatter.12.cloned.1.call-done = bf16[512,1536]{0,1:T(8,128)(2,1)} async-done(((bf16[2048,1536]{0,1:T(8,128)(2,1)}), bf16[512,1536]{0,1:T(8,128)(2,1)}) %reduce-scatter.12.cloned.1.call-update) | async-done | bytes 1572880 | tf_op jit(solution)/shard_map/reduce_scatter | solution.py:55
  320.1 1.8 pad_maximum_fusion.1
  321.9 4.8 %copy.43 = f32[512,3,2,384]{3,2,1,0:T(2,128)} copy(bf16[512,3,2,384]{0,3,2,1:T(8,128)(2,1)S(1)} %bitcast.23) | data formatting | bytes 7077888
  326.7 49.5 %reduce-scatter.10.cloned.1.call-done = bf16[128,2048]{1,0:T(8,128)(2,1)} async-done(((bf16[1024,2048]{1,0:T(8,128)(2,1)}), bf16[128,2048]{1,0:T(8,128)(2,1)}) %reduce-scatter.10.cloned.1.call-update) | async-done | bytes 524304 | tf_op jit(solution)/shard_map/reduce_scatter | solution.py:51
  376.2 55.3 %reduce-scatter.8.cloned.1.call-done = bf16[128,2048]{1,0:T(8,128)(2,1)} async-done(((bf16[1024,2048]{1,0:T(8,128)(2,1)}), bf16[128,2048]{1,0:T(8,128)(2,1)}) %reduce-scatter.8.cloned.1.call-update) | async-done | bytes 524304 | tf_op jit(solution)/shard_map/reduce_scatter | solution.py:41
  (36 shorter events, 3.9 us)
Async XLA Ops:
  7.2 42.2 %all-gather.3.cloned.1.call-start = ((), (), s32[]{:S(2)}) async-start(), calls=%async_computation.5 | async-start | bytes 4718592 | tf_op jit(solution)/shard_map/all_gather | solution.py:22
  7.9 80.1 %all-gather.5.cloned.1.call-start = ((), (), s32[]{:S(2)}) async-start(), calls=%async_computation.7 | async-start | bytes 4718592 | tf_op jit(solution)/shard_map/all_gather | solution.py:25
  8.6 145.5 %reduce-scatter.16.cloned.1.call-start = ((), (), s32[]{:S(2)}) async-start(), calls=%async_computation.11 | async-start | bytes 589824
  8.7 20.9 %copy-start.6 = (s32[128,4]{0,1:T(4,128)S(1)}, s32[128,4]{0,1:T(4,128)}, u32[]{:S(2)}) copy-start(s32[128,4]{0,1:T(4,128)} %param.6) | copy-start | bytes 6148
  8.7 20.9 %copy-start.7 = (f32[128,4]{0,1:T(4,128)S(1)}, f32[128,4]{0,1:T(4,128)}, u32[]{:S(2)}) copy-start(f32[128,4]{0,1:T(4,128)} %param.7) | copy-start | bytes 6148
  59.4 5.1 %copy-start = (f32[1024,1536]{1,0:T(8,128)}, f32[1024,1536]{1,0:T(8,128)S(1)}, u32[]{:S(2)}) copy-start(f32[1024,1536]{1,0:T(8,128)S(1)} %fusion.3) | copy-start | bytes 18874372
  106.7 3.2 copy-start.1
  109.6 97.4 %reduce-scatter.14.cloned.1.call-start = ((), (), s32[]{:S(2)}) async-start(), calls=%async_computation.10 | async-start | bytes 3932160 | tf_op jit(solution)/shard_map/reduce_scatter | solution.py:43
  109.9 7.2 %copy-start.8 = (bf16[1024,2048]{1,0:T(8,128)(2,1)S(1)}, bf16[1024,2048]{1,0:T(8,128)(2,1)}, u32[]{:S(2)}) copy-start(bf16[1024,2048]{1,0:T(8,128)(2,1)} %all-gather.5.cloned.1.call-done) | copy-start | bytes 12582916
  115.9 1.1 copy-start.2
  121.9 1.4 copy-start.4
  121.9 1.9 copy-start.5
  121.9 198.2 %reduce-scatter.12.cloned.1.call-start = ((), (), s32[]{:S(2)}) async-start(), calls=%async_computation.9 | async-start | bytes 7864320 | tf_op jit(solution)/shard_map/reduce_scatter | solution.py:55
  134.7 241.5 %reduce-scatter.10.cloned.1.call-start = ((), (), s32[]{:S(2)}) async-start(), calls=%async_computation.8 | async-start | bytes 4718592 | tf_op jit(solution)/shard_map/reduce_scatter | solution.py:51
  145.8 1.4 copy-start.3
  145.8 285.7 %reduce-scatter.8.cloned.1.call-start = ((), (), s32[]{:S(2)}) async-start(), calls=%async_computation.6 | async-start | bytes 4718592 | tf_op jit(solution)/shard_map/reduce_scatter | solution.py:41
Sparse Core Ops, SparseCore 0:
  9.9 39.4 all-gather.2
  51.3 36.6 all-gather.4
  109.8 34.1 reduce-scatter.15
  146.8 60.2 reduce-scatter.13
  209.3 110.7 reduce-scatter.11
  324.3 51.8 reduce-scatter.9
  380.1 51.3 reduce-scatter.7
where the time goes:
time: 439 us; the launch traced here: 438 us
  waiting for transfers between devices  294 us (67%)
  local copies, waits for them, and re-layouts  56.4 us (13%)
  matrix products  49.9 us (11%)
  between operations  14.3 us (3%)
  other arithmetic  12.8 us (3%)
  blocking collectives  10.5 us (2%)
    reduce_scatter x1, waiting for transfers between devices, local(): wgu_grad = lax.psum_scatter(wgu_grad, 'dp', scatter_dimension=0, tiled=True)  113 us
    reduce_scatter x1, waiting for transfers between devices, local(): lax.psum_scatter(lpart, 'expert', scatter_dimension=0, tiled=True)  55.3 us
    reduce_scatter x1, waiting for transfers between devices, local(): wd_grad = lax.psum_scatter(wd_grad, 'dp', scatter_dimension=0, tiled=True)  51.5 us
    dot_general x6, matrix products, dot(): lax.dot_general(a, b, (((ca,), (cb,)), ((), ())), preferred_element_type=...  49.9 us
    reduce_scatter x1, waiting for transfers between devices, local(): lax.psum_scatter(tpart, 'expert', scatter_dimension=0, tiled=True)  49.5 us
    reshape x1, local copies, waits for them, and re-layouts, local(): w = expert_weights.reshape(d, 3 * eh)  20.9 us
    unnamed x22, local copies, waits for them, and re-layouts  15.1 us
    all_gather x1, waiting for transfers between devices, local(): g = lax.all_gather(out_grad, 'expert', axis=0, tiled=True)  13.9 us
  transfers between devices with their start and end apart: 7, of which 6 were waited for; matrix products, arithmetic and copies ran while one was open for 21% of the time, Pallas kernels for 0%

commit v1 on v0

--- a/solution.py
+++ b/solution.py
@@ -19,9 +19,12 @@
     local_experts, h = expert_weights.shape[2:]
     n = ranks * tok_count
     eh = local_experts * h
-    x = lax.all_gather(tokens, "expert", axis=0, tiled=True)
     small = jnp.concatenate([expert_ids.astype(F32), gate_probs], axis=1)
-    small = lax.all_gather(small, "expert", axis=0, tiled=True)
+    x, small = jnp.split(
+        lax.all_gather(jnp.concatenate([tokens, small], axis=1), "expert", axis=0, tiled=True),
+        [tokens.shape[1]],
+        axis=1,
+    )
     g = lax.all_gather(out_grad, "expert", axis=0, tiled=True)
     ids = small[:, :top_count].astype(jnp.int32)
     probs = small[:, top_count:]

time: 439 us -> 474 us (1.080)
  waiting for transfers between devices: 294 us -> 327 us
  blocking collectives: 10.5 us -> 0 us
  local copies, waits for them, and re-layouts: 56.4 us -> 62 us
    all_gather x1, waiting for transfers between devices: 9.23 us -> 46.9 us  [local(): lax.all_gather(jnp.concatenate([tokens, small], axis=1), 'expert', axis=0...]
    all_gather x1 -> x0, blocking collectives: 10.5 us -> none  [local(): small = lax.all_gather(small, 'expert', axis=0, tiled=True)]
    convert_element_type x0 -> x1, local copies, waits for them, and re-layouts: none -> 6.45 us  [local(): weight_grad = wg.astype(F32).reshape(-1, 3, local_experts, h)]
    unnamed x22 -> x18, local copies, waits for them, and re-layouts: 15.1 us -> 11.4 us
  transfers between devices with their start and end apart: 7 -> 7, of which waited for: 6 -> 6; matrix products, arithmetic and copies ran while one was open for 21% -> 19% of each run, Pallas kernels for 0% -> 0%
where the time goes in v1:
time: 474 us; the launch traced here: 473 us
  waiting for transfers between devices  327 us (69%)
  local copies, waits for them, and re-layouts  62 us (13%)
  matrix products  52.7 us (11%)
  other arithmetic  16.6 us (4%)
  between operations  14.2 us (3%)
    reduce_scatter x1, waiting for transfers between devices, local(): wgu_grad = lax.psum_scatter(wgu_grad, 'dp', scatter_dimension=0, tiled=True)  113 us
    reduce_scatter x1, waiting for transfers between devices, local(): lax.psum_scatter(lpart, 'expert', scatter_dimension=0, tiled=True)  55.3 us
    dot_general x6, matrix products, dot(): lax.dot_general(a, b, (((ca,), (cb,)), ((), ())), preferred_element_type=...  52.7 us
    reduce_scatter x1, waiting for transfers between devices, local(): wd_grad = lax.psum_scatter(wd_grad, 'dp', scatter_dimension=0, tiled=True)  49.9 us
    all_gather x1, waiting for transfers between devices, local(): lax.all_gather(jnp.concatenate([tokens, small], axis=1), 'expert', axis=0...  46.9 us
    reduce_scatter x1, waiting for transfers between devices, local(): lax.psum_scatter(tpart, 'expert', scatter_dimension=0, tiled=True)  45.5 us
    reshape x1, local copies, waits for them, and re-layouts, local(): w = expert_weights.reshape(d, 3 * eh)  20.9 us
    all_gather x1, waiting for transfers between devices, local(): g = lax.all_gather(out_grad, 'expert', axis=0, tiled=True)  15.5 us
  transfers between devices with their start and end apart: 7, of which 6 were waited for; matrix products, arithmetic and copies ran while one was open for 19% of the time, Pallas kernels for 0%

profile of v1, /device:TPU:0, one launch (start us, length us, event | category | flops | bytes accessed | tf_op | source)
XLA Modules:
  0.0 473.0 jit_solution(226390186206413161)
XLA Ops:
  7.9 1.3 copy.42
  9.9 2.9 concatenate.9
  12.9 20.9 %reshape.38 = bf16[2048,2304]{1,0:T(8,128)(2,1)} reshape(bf16[2048,3,2,384]{3,2,1,0:T(2,128)(2,1)} %param.8) | data formatting | bytes 18874368 | tf_op jit(solution)/shard_map/reshape | solution.py:34
  33.8 15.5 %all-gather.5.cloned.1.call-done = bf16[1024,2048]{1,0:T(8,128)(2,1)} async-done(((bf16[128,2048]{1,0:T(8,128)(2,1)}), bf16[1024,2048]{1,0:T(8,128)(2,1)}) %all-gather.5.cloned.1.call-update) | async-done | bytes 4194320 | tf_op jit(solution)/shard_map/all_gather | solution.py:28
  49.3 6.3 %fusion.14 = f32[1024,768]{0,1:T(8,128)S(1)} fusion(bf16[1024,2048]{1,0:T(8,128)(2,1)} %all-gather.5.cloned.1.call-done, bf16[2048,2304]{1,0:T(8,128)(2,1)} %reshape.38), kind=kOutput, calls=%fused_computation.18 | convolution fusion | flops 3221225472 | bytes 10485760 | tf_op jit(solution)/shard_map/dot_general | solution.py:11
  55.6 2.4 copy.44
  58.1 2.4 copy.50
  60.4 46.9 %all-gather.3.cloned.1.call-done = f32[1024,2056]{0,1:T(8,128)} async-done(((f32[128,2056]{0,1:T(8,128)}), f32[1024,2056]{0,1:T(8,128)}) %all-gather.3.cloned.1.call-update) | async-done | bytes 8421392 | tf_op jit(solution)/shard_map/all_gather | solution.py:24
  107.3 11.3 %fusion.2 = f32[1024,1536]{1,0:T(8,128)S(1)} fusion(f32[1024,2056]{0,1:T(8,128)} %all-gather.3.cloned.1.call-done, bf16[2048,2304]{1,0:T(8,128)(2,1)} %reshape.38), kind=kOutput, calls=%fused_computation.2 | convolution fusion | flops 6442450944 | bytes 16777216 | tf_op jit(solution)/shard_map/dot_general | solution.py:11
  118.6 3.4 fusion.22
  122.0 1.3 copy-done
  123.3 2.4 copy.45
  125.7 2.5 copy.47
  128.2 2.4 copy.48
  130.6 2.3 copy.49
  132.9 4.8 %multiply_reduce_fusion = f32[1024,2]{0,1:T(2,128)S(1)} fusion(f32[1024,2,384]{2,0,1:T(8,128)} %copy.50, f32[1024,2,384]{2,0,1:T(8,128)} %copy.49, f32[1024,2,384]{2,0,1:T(8,128)} %copy.47), kind=kLoop, calls=%fused_computation.12 | loop fusion | flops 5502976 | bytes 9445376 | tf_op jit(solution)/shard_map/reduce_sum | solution.py:48
  138.9 2.4 mul.62
  141.3 1.9 copy.58
  144.5 6.0 %multiply_convert_fusion.1 = (bf16[1024,768]{1,0:T(8,128)(2,1)}, bf16[1024,768]{1,0:T(8,128)(2,1)}, bf16[1024,768]{1,0:T(8,128)(2,1)S(1)}) fusion(f32[1024,768]{1,0:T(8,128)} %bitcast.16, f32[1024,768]{1,0:T(8,128)S(1)} %copy-done.1, f32[1024,1536]{1,0:T(8,128)} %copy-done), kind=kLoop, calls=%fused_computation.14 | loop fusion | flops 14155776 | bytes 17301504 | tf_op jit(solution)/shard_map/convert_element_type | solution.py:50
  151.8 5.0 %fusion.13 = bf16[2048,768]{1,0:T(8,128)(2,1)} fusion(bf16[1024,768]{1,0:T(8,128)(2,1)S(1)} %get-tuple-element.8, bf16[1024,2048]{1,0:T(8,128)(2,1)S(1)} %copy-done.6), kind=kOutput, calls=%fused_computation.17 | convolution fusion | flops 3222798336 | bytes 8912896 | tf_op jit(solution)/shard_map/dot_general | solution.py:11
  156.9 1.3 copy-done.4
  158.7 12.1 %fusion.4 = bf16[2048,1536]{1,0:T(8,128)(2,1)} fusion(f32[1024,2056]{0,1:T(8,128)} %all-gather.3.cloned.1.call-done, bf16[1024,768]{1,0:T(8,128)(2,1)S(1)} %copy-done.5, bf16[1024,768]{1,0:T(8,128)(2,1)S(1)} %copy-done.4), kind=kOutput, calls=%fused_computation.4 | convolution fusion | flops 6448742400 | bytes 13631488 | tf_op jit(solution)/shard_map/dot_general | solution.py:11
  170.9 11.1 %fusion.10 = bf16[1024,2048]{1,0:T(8,128)(2,1)} fusion(bf16[2048,2304]{1,0:T(8,128)(2,1)} %reshape.38, bf16[1024,768]{1,0:T(8,128)(2,1)S(1)} %copy-done.5, bf16[1024,768]{1,0:T(8,128)(2,1)S(1)} %copy-done.4), kind=kOutput, calls=%fused_computation.8 | convolution fusion | flops 6450839552 | bytes 13631488 | tf_op jit(solution)/shard_map/dot_general | solution.py:11
  182.1 1.3 copy-done.3
  183.4 6.8 %convolution_convert_fusion = bf16[1024,2048]{1,0:T(8,128)(2,1)} fusion(bf16[1024,768]{1,0:T(8,128)(2,1)S(1)} %copy-done.3, bf16[2048,2304]{1,0:T(8,128)(2,1)} %reshape.38), kind=kOutput, calls=%fused_computation.9 | convolution fusion | flops 3223322624 | bytes 8912896 | tf_op jit(solution)/shard_map/dot_general | solution.py:11
  190.3 1.5 copy.56
  191.8 49.9 %reduce-scatter.14.cloned.1.call-done = bf16[512,768]{1,0:T(8,128)(2,1)} async-done(((bf16[2048,768]{1,0:T(8,128)(2,1)}), bf16[512,768]{1,0:T(8,128)(2,1)}) %reduce-scatter.14.cloned.1.call-update) | async-done | bytes 786448 | tf_op jit(solution)/shard_map/reduce_scatter | solution.py:46
  241.7 113.1 %reduce-scatter.12.cloned.1.call-done = bf16[512,1536]{1,0:T(8,128)(2,1)} async-done(((bf16[2048,1536]{1,0:T(8,128)(2,1)}), bf16[512,1536]{1,0:T(8,128)(2,1)}) %reduce-scatter.12.cloned.1.call-update) | async-done | bytes 1572880 | tf_op jit(solution)/shard_map/reduce_scatter | solution.py:58
  354.8 4.1 maximum_convert_fusion
  358.9 6.4 %reshape.42 = f32[512,3,2,384]{3,2,1,0:T(2,128)} reshape(f32[512,2304]{1,0:T(8,128)} %maximum_convert_fusion) | data formatting | bytes 9437184 | tf_op jit(solution)/shard_map/convert_element_type | solution.py:60
  365.4 45.5 %reduce-scatter.10.cloned.1.call-done = bf16[128,2048]{1,0:T(8,128)(2,1)} async-done(((bf16[1024,2048]{1,0:T(8,128)(2,1)}), bf16[128,2048]{1,0:T(8,128)(2,1)}) %reduce-scatter.10.cloned.1.call-update) | async-done | bytes 524304 | tf_op jit(solution)/shard_map/reduce_scatter | solution.py:54
  410.8 55.3 %reduce-scatter.8.cloned.1.call-done = bf16[128,2048]{1,0:T(8,128)(2,1)} async-done(((bf16[1024,2048]{1,0:T(8,128)(2,1)}), bf16[128,2048]{1,0:T(8,128)(2,1)}) %reduce-scatter.8.cloned.1.call-update) | async-done | bytes 524304 | tf_op jit(solution)/shard_map/reduce_scatter | solution.py:44
  (32 shorter events, 5.9 us)
Async XLA Ops:
  7.2 42.2 %all-gather.5.cloned.1.call-start = ((), (), s32[]{:S(2)}) async-start(), calls=%async_computation.7 | async-start | bytes 4718592 | tf_op jit(solution)/shard_map/all_gather | solution.py:28
  7.9 99.4 %all-gather.3.cloned.1.call-start = ((), (), s32[]{:S(2)}) async-start(), calls=%async_computation.5 | async-start | bytes 9474048 | tf_op jit(solution)/shard_map/all_gather | solution.py:24
  12.9 177.5 %reduce-scatter.16.cloned.1.call-start = ((), (), s32[]{:S(2)}) async-start(), calls=%async_computation.11 | async-start | bytes 589824
  118.6 4.7 copy-start
  141.3 3.2 copy-start.1
  144.3 97.4 %reduce-scatter.14.cloned.1.call-start = ((), (), s32[]{:S(2)}) async-start(), calls=%async_computation.10 | async-start | bytes 3932160 | tf_op jit(solution)/shard_map/reduce_scatter | solution.py:46
  144.5 7.2 %copy-start.6 = (bf16[1024,2048]{1,0:T(8,128)(2,1)S(1)}, bf16[1024,2048]{1,0:T(8,128)(2,1)}, u32[]{:S(2)}) copy-start(bf16[1024,2048]{1,0:T(8,128)(2,1)} %all-gather.5.cloned.1.call-done) | copy-start | bytes 12582916
  150.5 1.2 copy-start.2
  156.8 1.4 copy-start.4
  156.8 1.9 copy-start.5
  156.8 198.0 %reduce-scatter.12.cloned.1.call-start = ((), (), s32[]{:S(2)}) async-start(), calls=%async_computation.9 | async-start | bytes 7864320 | tf_op jit(solution)/shard_map/reduce_scatter | solution.py:58
  170.8 240.0 %reduce-scatter.10.cloned.1.call-start = ((), (), s32[]{:S(2)}) async-start(), calls=%async_computation.8 | async-start | bytes 4718592 | tf_op jit(solution)/shard_map/reduce_scatter | solution.py:54
  182.0 1.4 copy-start.3
  182.1 284.1 %reduce-scatter.8.cloned.1.call-start = ((), (), s32[]{:S(2)}) async-start(), calls=%async_computation.6 | async-start | bytes 4718592 | tf_op jit(solution)/shard_map/reduce_scatter | solution.py:44
Sparse Core Ops, SparseCore 0:
  9.9 39.4 all-gather.4
  51.2 56.0 all-gather.2
  144.4 34.1 reduce-scatter.15
  181.4 60.2 reduce-scatter.13
  244.0 110.7 reduce-scatter.11
  359.0 51.8 reduce-scatter.9
  414.8 51.2 reduce-scatter.7
